TPU v7x, 32 devices: a whole 2x2x4 slice. The times are simulated.
32 devices in a mesh: occ: 16 (over z, y, core), vir: 2 (over x).
Axes of the slice: x: 2, y: 2, z: 4, core: 2. Of those that a mesh axis runs over, the one named last changes fastest.
Arguments:
- lambda_triples: bfloat16 [256, 320, 320], P('occ', 'vir'), may hold values from -6 to 6
- amplitude_triples: bfloat16 [256, 320, 320], P('occ', 'vir'), may hold values from -6 to 6
- spin_extent: int32 [256], P('occ'), may hold values from 80 to 320
- ladder_weight: bfloat16 [320, 320], P(None, 'vir'), may hold values from -0.3125 to 0.3125
- cycle_weight: bfloat16 [320, 40], replicated, may hold values from -0.3125 to 0.3125
- lambda_doubles: bfloat16 [40, 320], P(None, 'vir'), may hold values from -1 to 1
Outputs:
- residual: bfloat16 [256, 320, 320], P('occ', 'vir')
All inputs are finite; a program needn't handle non-finite values.
Results may differ from a plain program's by a relative error of at most 0.0043.
Values may be sent and summed in bfloat16 or wider, within the bound.
No kernel may reach another device: no remote copies, remote signals or barrier semaphores. Data moves between devices by JAX's collectives and lax.ppermute only.
A program may use at most 64 MiB of HBM per device.

v0:
```python
import jax
import jax.numpy as jnp
from jax import lax
from jax.sharding import PartitionSpec as P


def on_device(
    lambda_triples, amplitude_triples, spin_extent, ladder_weight, cycle_weight, lambda_doubles
):
    f32 = jnp.float32
    width = lambda_triples.shape[2]
    triples_all = lambda_triples.shape[0] * lax.axis_size("occ")
    columns = jnp.arange(width, dtype=jnp.int32)
    keep = columns[None, :] < spin_extent[:, None]
    masked = jnp.where(keep[:, None, :], lambda_triples, jnp.zeros_like(lambda_triples))
    ladder_full, doubles_full = (
        lax.all_gather(ladder_weight, "vir", axis=1, tiled=True),
        lax.all_gather(lambda_doubles, "vir", axis=1, tiled=True),
    )
    ladder_term = jnp.einsum("tae,eb->tab", masked, ladder_full, preferred_element_type=f32)
    cycle_mid = jnp.einsum(
        "tae,em->tam", amplitude_triples, cycle_weight, preferred_element_type=f32
    ).astype(jnp.bfloat16)
    cycle_term = jnp.einsum("tam,mb->tab", cycle_mid, doubles_full, preferred_element_type=f32)
    partial_density = jnp.einsum(
        "tae,tbe->ab",
        masked,
        lax.all_gather(amplitude_triples, "vir", axis=1, tiled=True),
        preferred_element_type=f32,
    )
    density = lax.psum(partial_density, "occ")
    density = (density / jnp.sqrt(f32(triples_all * width))).astype(jnp.bfloat16)
    density_term = jnp.einsum(
        "ac,tcb->tab",
        density,
        lax.all_gather(masked, "vir", axis=1, tiled=True),
        preferred_element_type=f32,
    )
    density_term = density_term / jnp.sqrt(f32(width))
    return (ladder_term + cycle_term + density_term).astype(jnp.bfloat16)


def solution(mesh):
    return jax.shard_map(
        on_device,
        mesh=mesh,
        in_specs=(
            P("occ", "vir", None),
            P("occ", "vir", None),
            P("occ"),
            P(None, "vir"),
            P(),
            P(None, "vir"),
        ),
        out_specs=P("occ", "vir", None),
        check_vma=False,
    )
```

profile of v0, /device:TPU:8, one launch (start us, length us, event | category | flops | bytes accessed | tf_op | source)
XLA Modules:
  0.0 227.4 jit_solution(11360172198900712387)
XLA Ops:
  6.5 0.0 copy-start
  6.5 0.0 copy-start.3
  6.5 0.0 copy-start.2
  6.5 0.0 all-gather.6.cloned.1.call-start
  6.5 0.7 all-gather.6.cloned.1.call-update
  7.3 0.0 all-gather.4.cloned.1.call-start
  7.3 0.7 iota_compare_fusion
  8.0 3.0 %broadcast_select_fusion = bf16[16,160,320]{2,1,0:T(8,128)(2,1)} fusion(bf16[16,160,320]{2,1,0:T(8,128)(2,1)} %param.6, pred[16,320]{1,0:T(8,128)(4,1)S(1)} %iota_compare_fusion), kind=kLoop, calls=%fused_computation.2 | loop fusion | flops 819200 | bytes 3281920 | tf_op jit(solution)/shard_map/jit(_where)/select_n | solution.py:15
  11.1 0.0 copy-start.1
  11.1 0.0 all-gather.4.cloned.1.call-update
  11.1 0.0 all-reduce.2.cloned.1.call-start
  11.2 0.0 copy-done.3
  11.2 4.6 %all-gather = bf16[2,160,40]{1,2,0:T(8,128)(2,1)S(1)} all-gather(bf16[1,160,40]{1,2,0:T(8,128)(2,1)S(1)} %bitcast.27), channel_id=1, replica_groups=mesh['occ'=16,'vir'=2] {'vir'}, dimensions={0}, use_global_device_ids=true | all-gather | bytes 38400 | tf_op jit(solution)/shard_map/all_gather | solution.py:18
  15.8 0.1 reshape.21
  15.9 0.0 copy-done.2
  15.9 6.4 %all_gather.12 = bf16[320,320]{0,1:T(8,128)(2,1)S(1)} all-gather(bf16[320,160]{0,1:T(8,128)(2,1)S(1)} %copy-done.2), channel_id=1, replica_groups=mesh['occ'=16,'vir'=2] {'vir'}, dimensions={1}, use_global_device_ids=true | all-gather | bytes 307200 | tf_op jit(solution)/shard_map/all_gather | solution.py:17
  22.3 4.9 %fusion.2 = f32[16,160,320]{2,1,0:T(8,128)} fusion(bf16[16,160,320]{2,1,0:T(8,128)(2,1)} %broadcast_select_fusion, bf16[320,320]{0,1:T(8,128)(2,1)S(1)} %all_gather.12), kind=kOutput, calls=%fused_computation.6 | convolution fusion | flops 524288000 | bytes 5120000 | tf_op jit(solution)/shard_map/tae,eb->tab/dot_general | solution.py:20
  27.2 36.7 %all-gather.6.cloned.1.call-done = bf16[16,320,320]{2,1,0:T(8,128)(2,1)} async-done(((bf16[16,160,320]{2,1,0:T(8,128)(2,1)}), bf16[16,320,320]{2,1,0:T(8,128)(2,1)}) %all-gather.6.cloned.1.call-update) | async-done | bytes 3276816 | tf_op jit(solution)/shard_map/all_gather | solution.py:28
  63.9 0.0 copy-done.1
  63.9 4.4 %convolution_bitcast_fusion = f32[160,320]{1,0:T(8,128)} fusion(bf16[16,160,320]{2,1,0:T(8,128)(2,1)S(1)} %copy-done.1, bf16[16,320,320]{2,1,0:T(8,128)(2,1)} %all-gather.6.cloned.1.call-done), kind=kOutput, calls=%fused_computation.5 | convolution fusion | flops 524288000 | bytes 5120000 | tf_op jit(solution)/shard_map/tae,tbe->ab/dot_general | solution.py:25
  68.3 0.0 all-reduce.2.cloned.1.call-update
  68.3 0.0 copy-done
  68.3 5.2 %fusion.1 = f32[16,160,320]{2,1,0:T(8,128)} fusion(bf16[320,40,1]{0,1,2:T(8,128)(2,1)S(1)} %reshape.21, bf16[16,160,320]{2,1,0:T(8,128)(2,1)} %param.7, bf16[320,40]{0,1:T(8,128)(2,1)S(1)} %copy-done), kind=kOutput, calls=%fused_computation.4 | convolution fusion | flops 131174400 | bytes 4966400 | tf_op jit(solution)/shard_map/tam,mb->tab/dot_general | solution.py:24
  73.5 46.9 %all-gather.4.cloned.1.call-done = bf16[16,320,320]{2,1,0:T(8,128)(2,1)} async-done(((bf16[16,160,320]{2,1,0:T(8,128)(2,1)}), bf16[16,320,320]{2,1,0:T(8,128)(2,1)}) %all-gather.4.cloned.1.call-update) | async-done | bytes 3276816 | tf_op jit(solution)/shard_map/all_gather | solution.py:36
  120.4 93.5 %all-reduce.2.cloned.1.call-done = f32[160,320]{1,0:T(8,128)} async-done(((f32[160,320]{1,0:T(8,128)}), f32[160,320]{1,0:T(8,128)}) %all-reduce.2.cloned.1.call-update) | async-done | bytes 204816 | tf_op jit(solution)/shard_map/psum | solution.py:31
  213.9 7.0 %fusion = bf16[16,160,320]{2,1,0:T(8,128)(2,1)} fusion(f32[16,160,320]{2,1,0:T(8,128)} %fusion.2, f32[16,160,320]{2,1,0:T(8,128)} %fusion.1, bf16[16,320,320]{2,1,0:T(8,128)(2,1)} %all-gather.4.cloned.1.call-done, f32[160,320]{1,0:T(8,128)} %all-reduce.2.cloned.1.call-done), kind=kOutput, calls=%fused_computation.1 | convolution fusion | flops 527667200 | bytes 11673600 | tf_op jit(solution)/shard_map/ac,tcb->tab/dot_general | solution.py:33
  (1 shorter events, 0.0 us)
Async XLA Ops:
  6.5 61.8 %copy-start = (bf16[320,40]{0,1:T(8,128)(2,1)S(1)}, bf16[320,40]{0,1:T(8,128)(2,1)}, u32[]{:S(2)}) copy-start(bf16[320,40]{0,1:T(8,128)(2,1)} %param.10) | copy-start | bytes 76804
  6.5 4.6 %copy-start.3 = (bf16[40,160]{1,0:T(8,128)(2,1)S(1)}, bf16[40,160]{1,0:T(8,128)(2,1)}, u32[]{:S(2)}) copy-start(bf16[40,160]{1,0:T(8,128)(2,1)} %param.11) | copy-start | bytes 38404
  6.5 9.4 %copy-start.2 = (bf16[320,160]{0,1:T(8,128)(2,1)S(1)}, bf16[320,160]{0,1:T(8,128)(2,1)}, u32[]{:S(2)}) copy-start(bf16[320,160]{0,1:T(8,128)(2,1)} %param.9) | copy-start | bytes 307204
  6.5 57.4 %all-gather.6.cloned.1.call-start = ((), (), s32[]{:S(2)}) async-start(), calls=%async_computation.1 | async-start | bytes 5898240 | tf_op jit(solution)/shard_map/all_gather | solution.py:28
  7.3 113.1 %all-gather.4.cloned.1.call-start = ((), (), s32[]{:S(2)}) async-start(), calls=%async_computation | async-start | bytes 5898240 | tf_op jit(solution)/shard_map/all_gather | solution.py:36
  11.1 52.8 %copy-start.1 = (bf16[16,160,320]{2,1,0:T(8,128)(2,1)S(1)}, bf16[16,160,320]{2,1,0:T(8,128)(2,1)}, u32[]{:S(2)}) copy-start(bf16[16,160,320]{2,1,0:T(8,128)(2,1)} %broadcast_select_fusion) | copy-start | bytes 4915204
  11.1 202.8 %all-reduce.2.cloned.1.call-start = ((), (), s32[]{:S(2)}) async-start(), calls=%async_computation.2 | async-start | bytes 491520 | tf_op jit(solution)/shard_map/psum | solution.py:31
Sparse Core Ops, SparseCore 0:
  8.9 54.9 all-gather.5
  65.4 54.8 all-gather.3
  123.8 90.0 all-reduce.1
where the time goes:
time: 228 us; the launch traced here: 227 us
  waiting for transfers between devices  178 us (78%)
  matrix products  21.4 us (9%)
  between operations  13.1 us (6%)
  blocking collectives  11 us (5%)
  other arithmetic  3.77 us (2%)
    psum x1, waiting for transfers between devices, on_device(): density = lax.psum(partial_density, 'occ')  93.5 us
    all_gather x1, waiting for transfers between devices, on_device(): lax.all_gather(masked, 'vir', axis=1, tiled=True)  46.9 us
    all_gather x1, waiting for transfers between devices, on_device(): lax.all_gather(amplitude_triples, 'vir', axis=1, tiled=True)  36.7 us
    dot_general x1, matrix products, on_device(): jnp.einsum('ac,tcb->tab', density, lax.all_gather(masked, 'vir', axis=1,...  6.97 us
    all_gather x1, blocking collectives, on_device(): lax.all_gather(ladder_weight, 'vir', axis=1, tiled=True)  6.43 us
    dot_general x1, matrix products, on_device(): jnp.einsum('tam,mb->tab', cycle_mid, doubles_full, preferred_element_type...  5.16 us
    dot_general x1, matrix products, on_device(): jnp.einsum('tae,eb->tab', masked, ladder_full, preferred_element_type=f32)  4.91 us
    all_gather x1, blocking collectives, on_device(): lax.all_gather(lambda_doubles, 'vir', axis=1, tiled=True)  4.59 us
  transfers between devices with their start and end apart: 3, of which 3 were waited for; matrix products, arithmetic and copies ran while one was open for 8% of the time, Pallas kernels for 0%

commit v1 on v0

--- a/solution.py
+++ b/solution.py
@@ -2,6 +2,25 @@
 import jax.numpy as jnp
 from jax import lax
 from jax.sharding import PartitionSpec as P
+
+
+def joined_along(tiles, dim):
+    dims = list(tiles.shape[1:])
+    dims[dim] *= tiles.shape[0]
+    return jnp.moveaxis(tiles, 0, dim).reshape(dims)
+
+
+def work_around(shard, axis, dim, work, out_dim):
+    devices, position, span = (lax.axis_size(axis), lax.axis_index(axis), shard.shape[dim])
+    right = [(i, (i + 1) % devices) for i in range(devices)]
+    tiles = []
+    current = shard
+    for step in range(devices):
+        coming = current if step == devices - 1 else lax.ppermute(current, axis, right)
+        tiles.append(work(current, (position - step) % devices * span))
+        current = coming
+    tiles = jnp.stack(tiles)[(position - jnp.arange(devices)) % devices]
+    return joined_along(tiles, out_dim)
 
 
 def on_device(
@@ -22,11 +41,14 @@
         "tae,em->tam", amplitude_triples, cycle_weight, preferred_element_type=f32
     ).astype(jnp.bfloat16)
     cycle_term = jnp.einsum("tam,mb->tab", cycle_mid, doubles_full, preferred_element_type=f32)
-    partial_density = jnp.einsum(
-        "tae,tbe->ab",
-        masked,
-        lax.all_gather(amplitude_triples, "vir", axis=1, tiled=True),
-        preferred_element_type=f32,
+    partial_density = work_around(
+        amplitude_triples,
+        "vir",
+        1,
+        lambda own_block, start: jnp.einsum(
+            "tae,tbe->ab", masked, own_block, preferred_element_type=f32
+        ),
+        1,
     )
     density = lax.psum(partial_density, "occ")
     density = (density / jnp.sqrt(f32(triples_all * width))).astype(jnp.bfloat16)

time: 228 us -> 163 us (0.71)
  waiting for transfers between devices: 178 us -> 110 us
    all_gather x1, waiting for transfers between devices: 46.9 us -> 0.01 us  [on_device(): lax.all_gather(masked, 'vir', axis=1, tiled=True)]
    ppermute x0 -> x1, waiting for transfers between devices: none -> 37.9 us  [work_around(): lax.ppermute(current, axis, right)]
    all_gather x1 -> x0, waiting for transfers between devices: 36.7 us -> none  [on_device(): lax.all_gather(amplitude_triples, 'vir', axis=1, tiled=True)]
    psum x1, waiting for transfers between devices: 93.5 us -> 71.9 us  [on_device(): density = lax.psum(partial_density, 'occ')]
    dot_general x1 -> x2, matrix products: 4.41 us -> 5.17 us  [on_device(): jnp.einsum('tae,tbe->ab', masked, own_block, preferred_element_type=f32)]
  transfers between devices with their start and end apart: 3 -> 3, of which waited for: 3 -> 2; matrix products, arithmetic and copies ran while one was open for 8% -> 9% of each run, Pallas kernels for 0% -> 0%
where the time goes in v1:
time: 163 us; the launch traced here: 162 us
  waiting for transfers between devices  110 us (67%)
  matrix products  21 us (13%)
  between operations  14.9 us (9%)
  blocking collectives  10 us (6%)
  other arithmetic  2.55 us (2%)
  local copies, waits for them, and re-layouts  1.92 us (1%)
    psum x1, waiting for transfers between devices, on_device(): density = lax.psum(partial_density, 'occ')  71.9 us
    ppermute x1, waiting for transfers between devices, work_around(): lax.ppermute(current, axis, right)  37.9 us
    dot_general x1, matrix products, on_device(): jnp.einsum('ac,tcb->tab', density, lax.all_gather(masked, 'vir', axis=1,...  6.99 us
    dot_general x1, matrix products, on_device(): jnp.einsum('tam,mb->tab', cycle_mid, doubles_full, preferred_element_type...  5.64 us
    all_gather x1, blocking collectives, on_device(): lax.all_gather(ladder_weight, 'vir', axis=1, tiled=True)  5.56 us
    dot_general x2, matrix products, on_device(): jnp.einsum('tae,tbe->ab', masked, own_block, preferred_element_type=f32)  5.17 us
    all_gather x1, blocking collectives, on_device(): lax.all_gather(lambda_doubles, 'vir', axis=1, tiled=True)  4.46 us
  transfers between devices with their start and end apart: 3, of which 2 were waited for; matrix products, arithmetic and copies ran while one was open for 9% of the time, Pallas kernels for 0%

profile of v1, /device:TPU:8, one launch (start us, length us, event | category | flops | bytes accessed | tf_op | source)
XLA Modules:
  0.0 162.3 jit_solution(16166245806487901272)
XLA Ops:
  7.4 0.0 copy-start
  7.4 0.0 all-reduce.2.cloned.1.call-start
  7.4 1.5 collective-permute-start
  8.9 0.7 iota_compare_fusion
  9.6 1.8 %broadcast_select_fusion = bf16[16,160,320]{2,1,0:T(8,128)(2,1)S(1)} fusion(bf16[16,160,320]{2,1,0:T(8,128)(2,1)} %param.6, pred[16,320]{1,0:T(8,128)(4,1)S(1)} %iota_compare_fusion), kind=kLoop, calls=%fused_computation.3 | loop fusion | flops 819200 | bytes 3281920 | tf_op jit(solution)/shard_map/jit(_where)/select_n | solution.py:34
  11.4 0.0 copy-start.1
  11.4 2.9 %convolution_bitcast_fusion.1 = f32[1,160,160]{2,1,0:T(8,128)S(1)} fusion(bf16[16,160,320]{2,1,0:T(8,128)(2,1)S(1)} %broadcast_select_fusion, bf16[16,160,320]{2,1,0:T(8,128)(2,1)} %param.7), kind=kOutput, calls=%fused_computation.7 | convolution fusion | flops 262144000 | bytes 3379200 | tf_op jit(solution)/shard_map/tae,tbe->ab/dot_general | solution.py:48
  14.4 37.9 %collective-permute-done = bf16[16,160,320]{2,1,0:T(8,128)(2,1)} collective-permute-done((bf16[16,160,320]{2,1,0:T(8,128)(2,1)}, bf16[16,160,320]{2,1,0:T(8,128)(2,1)}, u32[]{:S(2)}, u32[]{:S(2)}) %collective-permute-start) | collective-permute-done | bytes 1638432 | tf_op jit(solution)/shard_map/ppermute | solution.py:19
  52.2 0.0 copy-done.1
  52.3 2.2 %convolution_bitcast_fusion = f32[1,160,160]{2,1,0:T(8,128)S(1)} fusion(bf16[16,160,320]{2,1,0:T(8,128)(2,1)S(1)} %broadcast_select_fusion, bf16[16,160,320]{2,1,0:T(8,128)(2,1)} %collective-permute-done), kind=kOutput, calls=%fused_computation.6 | convolution fusion | flops 262144000 | bytes 3379200 | tf_op jit(solution)/shard_map/tae,tbe->ab/dot_general | solution.py:48
  54.5 0.0 copy-start.4
  54.5 0.6 gather_fusion
  55.1 0.0 copy-start.3
  55.1 0.3 copy.11
  55.4 0.9 reshape.69
  56.3 0.0 all-reduce.2.cloned.1.call-update
  56.3 0.0 all-gather.3.cloned.1.call-start
  56.4 0.5 all-gather.3.cloned.1.call-update
  56.9 0.0 copy-done.4
  56.9 4.5 %all-gather = bf16[2,160,40]{1,2,0:T(8,128)(2,1)S(1)} all-gather(bf16[1,160,40]{1,2,0:T(8,128)(2,1)S(1)} %bitcast.37), channel_id=1, replica_groups=mesh['occ'=16,'vir'=2] {'vir'}, dimensions={0}, use_global_device_ids=true | all-gather | bytes 38400 | tf_op jit(solution)/shard_map/all_gather | solution.py:37
  61.4 0.1 reshape.82
  61.5 0.0 copy-done.3
  61.5 5.6 %all_gather.9 = bf16[320,320]{0,1:T(8,128)(2,1)S(1)} all-gather(bf16[320,160]{0,1:T(8,128)(2,1)S(1)} %copy-done.3), channel_id=1, replica_groups=mesh['occ'=16,'vir'=2] {'vir'}, dimensions={1}, use_global_device_ids=true | all-gather | bytes 307200 | tf_op jit(solution)/shard_map/all_gather | solution.py:36
  67.1 0.0 copy-done
  67.1 0.0 copy-start.2
  67.1 5.6 %fusion.1 = f32[16,160,320]{2,1,0:T(8,128)} fusion(bf16[320,40,1]{0,1,2:T(8,128)(2,1)S(1)} %reshape.82, bf16[16,160,320]{2,1,0:T(8,128)(2,1)} %param.7, bf16[320,40]{0,1:T(8,128)(2,1)S(1)} %copy-done), kind=kOutput, calls=%fused_computation.5 | convolution fusion | flops 131174400 | bytes 4966400 | tf_op jit(solution)/shard_map/tam,mb->tab/dot_general | solution.py:43
  72.7 0.0 copy-done.2
  72.7 3.2 %fusion.2 = f32[16,160,320]{2,1,0:T(8,128)} fusion(bf16[16,160,320]{2,1,0:T(8,128)(2,1)S(1)} %copy-done.2, bf16[320,320]{0,1:T(8,128)(2,1)S(1)} %all_gather.9), kind=kOutput, calls=%fused_computation.9 | convolution fusion | flops 524288000 | bytes 5120000 | tf_op jit(solution)/shard_map/tae,eb->tab/dot_general | solution.py:39
  76.0 71.9 %all-reduce.2.cloned.1.call-done = f32[160,320]{1,0:T(8,128)} async-done(((f32[160,320]{1,0:T(8,128)}), f32[160,320]{1,0:T(8,128)}) %all-reduce.2.cloned.1.call-update) | async-done | bytes 204816 | tf_op jit(solution)/shard_map/psum | solution.py:53
  147.9 0.0 all-gather.3.cloned.1.call-done
  147.9 7.0 %fusion = bf16[16,160,320]{2,1,0:T(8,128)(2,1)} fusion(f32[16,160,320]{2,1,0:T(8,128)} %fusion.2, f32[16,160,320]{2,1,0:T(8,128)} %fusion.1, bf16[16,320,320]{2,1,0:T(8,128)(2,1)} %all-gather.3.cloned.1.call-done, f32[160,320]{1,0:T(8,128)} %all-reduce.2.cloned.1.call-done), kind=kOutput, calls=%fused_computation.2 | convolution fusion | flops 527667200 | bytes 11673600 | tf_op jit(solution)/shard_map/ac,tcb->tab/dot_general | solution.py:55
  (4 shorter events, 0.1 us)
Async XLA Ops:
  7.4 59.7 %copy-start = (bf16[320,40]{0,1:T(8,128)(2,1)S(1)}, bf16[320,40]{0,1:T(8,128)(2,1)}, u32[]{:S(2)}) copy-start(bf16[320,40]{0,1:T(8,128)(2,1)} %param.10) | copy-start | bytes 76804
  7.4 140.5 %all-reduce.2.cloned.1.call-start = ((), (), s32[]{:S(2)}) async-start(), calls=%async_computation.1 | async-start | bytes 491520 | tf_op jit(solution)/shard_map/psum | solution.py:53
  7.4 44.9 %collective-permute-start = (bf16[16,160,320]{2,1,0:T(8,128)(2,1)}, bf16[16,160,320]{2,1,0:T(8,128)(2,1)}, u32[]{:S(2)}, u32[]{:S(2)}) collective-permute-start(bf16[16,160,320]{2,1,0:T(8,128)(2,1)} %param.7), channel_id=1, source_target_pairs={{0,1},{1,0},{2,3},{3,2},{4,5},{5,4},{6,7},{7,6},{8,9},{9,8},{10,11... | collective-permute-start | bytes 4915208 | tf_op jit(solution)/shard_map/ppermute | solution.py:19
  11.4 40.9 %copy-start.1 = (bf16[16,160,320]{2,1,0:T(8,128)(2,1)}, bf16[16,160,320]{2,1,0:T(8,128)(2,1)S(1)}, u32[]{:S(2)}) copy-start(bf16[16,160,320]{2,1,0:T(8,128)(2,1)S(1)} %broadcast_select_fusion) | copy-start | bytes 4915204
  54.5 2.4 %copy-start.4 = (bf16[40,160]{1,0:T(8,128)(2,1)S(1)}, bf16[40,160]{1,0:T(8,128)(2,1)}, u32[]{:S(2)}) copy-start(bf16[40,160]{1,0:T(8,128)(2,1)} %param.11) | copy-start | bytes 38404
  55.1 6.4 %copy-start.3 = (bf16[320,160]{0,1:T(8,128)(2,1)S(1)}, bf16[320,160]{0,1:T(8,128)(2,1)}, u32[]{:S(2)}) copy-start(bf16[320,160]{0,1:T(8,128)(2,1)} %param.9) | copy-start | bytes 307204
  56.3 91.5 %all-gather.3.cloned.1.call-start = ((), (), s32[]{:S(2)}) async-start(), calls=%async_computation | async-start | bytes 5898240 | tf_op jit(solution)/shard_map/all_gather | solution.py:58
  67.1 5.6 %copy-start.2 = (bf16[16,160,320]{2,1,0:T(8,128)(2,1)S(1)}, bf16[16,160,320]{2,1,0:T(8,128)(2,1)}, u32[]{:S(2)}) copy-start(bf16[16,160,320]{2,1,0:T(8,128)(2,1)} %copy-done.1) | copy-start | bytes 4915204
Sparse Core Ops, SparseCore 0:
  56.5 91.3 all-reduce.1
Sparse Core Ops, SparseCore 1:
  58.4 54.8 all-gather.2
